TPU v7x, 32 devices: a whole 2x2x4 slice. The times are simulated.
32 devices in a mesh: req: 8 (over y, x, core), cand: 4 (over z).
Axes of the slice: x: 2, y: 2, z: 4, core: 2. Of those that a mesh axis runs over, the one named last changes fastest.
Arguments:
- history: bfloat16 [64, 256, 1024], P('req', 'cand'), may hold values from -6 to 6
- history_length: int32 [64], P('req'), may hold values from 32 to 256
- candidate_count: int32 [64], P('req'), may hold values from 512 to 4096
- block_shard: int32 [64, 32], P('req'), may hold values from 0 to 3, as said below
- block_index: int32 [64, 32], P('req'), may hold values from 0 to 3
- item_table: bfloat16 [16, 128, 1024], P('cand'), may hold values from -6 to 6
- item_ages: int32 [64, 4096], P('req', 'cand'), may hold values from 0 to 336
- history_weight: bfloat16 [1024, 2048], P('req'), may hold values from -0.1875 to 0.1875
- candidate_weight: bfloat16 [1024, 2048], P('req'), may hold values from -0.1875 to 0.1875
- output_weight: bfloat16 [1024, 1024], P('req'), may hold values from -0.1875 to 0.1875
- hidden_weight: bfloat16 [1024, 256], P('req'), may hold values from -0.1875 to 0.1875
- norm_gain: float32 [1024], replicated, may hold values from 0.1 to 1.9
- score_weight: bfloat16 [2, 256], replicated, may hold values from -0.375 to 0.375
Outputs:
- scores: float32 [64, 4096], P('req', 'cand')
Inputs may be any that keep to these rules, and one draw needn't show every extreme that they name: `block_shard`: for each group of 8 consecutive requests (aligned) and each c, the slots j with j // 8 == c of those requests name every shard exactly 16 times.
All inputs are finite; a program needn't handle non-finite values.
Results may differ from a plain program's by a relative error of at most 0.0053.
Values may be sent and summed in bfloat16 or wider, within the bound.
A program may use at most 128 MiB of HBM per device.

v0:
```python
import math
import jax
import jax.numpy as jnp
from jax import lax
from jax.sharding import PartitionSpec as P

HEADS = 8
BLOCK = 128
EPSILON = 1e-05
AGE_SCALE = 48.0


def local(
    history,
    history_length,
    candidate_count,
    block_shard,
    block_index,
    item_table,
    item_ages,
    history_weight,
    candidate_weight,
    output_weight,
    hidden_weight,
    norm_gain,
    score_weight,
):
    proj_history, proj_candidate, proj_output, proj_hidden = (
        lax.all_gather(history_weight, "req", axis=0, tiled=True),
        lax.all_gather(candidate_weight, "req", axis=0, tiled=True),
        lax.all_gather(output_weight, "req", axis=0, tiled=True),
        lax.all_gather(hidden_weight, "req", axis=0, tiled=True),
    )
    shards = lax.axis_size("cand")
    my_shard = lax.axis_index("cand")
    requests, max_blocks = block_shard.shape
    per_scorer = max_blocks // shards
    slot_count = requests * per_scorer
    capacity = slot_count // shards
    model_width = item_table.shape[2]
    head_size = model_width // HEADS
    score_scale = 1.0 / math.sqrt(head_size)
    shard_sets = (
        block_shard.reshape(requests, shards, per_scorer)
        .transpose(1, 0, 2)
        .reshape(shards, slot_count)
    )
    index_sets = (
        block_index.reshape(requests, shards, per_scorer)
        .transpose(1, 0, 2)
        .reshape(shards, slot_count)
    )
    is_mine = (shard_sets == my_shard).astype(jnp.int32)
    before = jnp.cumsum(is_mine, axis=1) - is_mine
    picked = is_mine[:, None, :] * (
        before[:, None, :] == jnp.arange(capacity, dtype=jnp.int32)[None, :, None]
    ).astype(jnp.int32)
    send_ids = jnp.sum(picked * index_sets[:, None, :], axis=2)
    outgoing = item_table[send_ids]
    incoming = lax.all_to_all(outgoing, "cand", split_axis=0, concat_axis=0, tiled=True)
    own_shard = lax.dynamic_index_in_dim(shard_sets, my_shard, 0, keepdims=False)
    matches = (own_shard[:, None] == jnp.arange(shards, dtype=jnp.int32)[None, :]).astype(jnp.int32)
    own_rank = jnp.sum((jnp.cumsum(matches, axis=0) - matches) * matches, axis=1)
    arrived = incoming.reshape(shards * capacity, BLOCK, model_width)[
        own_shard * capacity + own_rank
    ]
    arrived = arrived.reshape(requests, per_scorer, BLOCK, model_width)
    first_block = jnp.zeros((requests,), jnp.int32) + my_shard * per_scorer
    block_number = first_block[:, None] + jnp.arange(per_scorer, dtype=jnp.int32)[None, :]
    live_slots = (block_number * BLOCK < candidate_count[:, None]).reshape(slot_count)
    request_of = jnp.arange(slot_count, dtype=jnp.int32) // per_scorer
    local_pairs = jax.nn.silu(
        jnp.dot(history.reshape(-1, model_width), proj_history, preferred_element_type=jnp.float32)
    ).astype(jnp.bfloat16)
    local_pairs = local_pairs.reshape(requests, -1, 2 * model_width)
    projected = lax.all_gather(local_pairs, "cand", axis=1, tiled=True)
    history_total = projected.shape[1]
    positions = jnp.arange(history_total, dtype=jnp.int32)
    query_weight = proj_candidate[:, :model_width]
    gate_weight = proj_candidate[:, model_width:]

    def score_slot(operands):
        block_rows, request, is_live = operands

        def score_block(block_rows):
            query = jax.nn.silu(
                jnp.dot(block_rows, query_weight, preferred_element_type=jnp.float32)
            ).astype(jnp.bfloat16)
            query = query.reshape(BLOCK, HEADS, head_size)
            pair_rows = lax.dynamic_index_in_dim(projected, request, 0, keepdims=False)
            key_rows = pair_rows[:, :model_width].reshape(history_total, HEADS, head_size)
            value_rows = pair_rows[:, model_width:].reshape(history_total, HEADS, head_size)
            length = lax.dynamic_index_in_dim(history_length, request, 0, keepdims=False)
            scores = (
                jnp.einsum("ihd,phd->hip", query, key_rows, preferred_element_type=jnp.float32)
                * score_scale
            )
            weights = jax.nn.silu(scores) / length.astype(jnp.float32)
            weights = jnp.where(positions[None, None, :] < length, weights, 0.0).astype(
                jnp.bfloat16
            )
            attended = jnp.einsum(
                "hip,phd->ihd", weights, value_rows, preferred_element_type=jnp.float32
            ).reshape(BLOCK, model_width)
            gate = jax.nn.silu(jnp.dot(block_rows, gate_weight, preferred_element_type=jnp.float32))
            center = attended - jnp.mean(attended, axis=-1, keepdims=True)
            spread = jnp.mean(center * center, axis=-1, keepdims=True)
            normed = (center * lax.rsqrt(spread + EPSILON) * norm_gain * gate).astype(jnp.bfloat16)
            merged = (
                jnp.dot(normed, proj_output, preferred_element_type=jnp.float32)
                + block_rows.astype(jnp.float32)
            ).astype(jnp.bfloat16)
            hidden = jax.nn.silu(
                jnp.dot(merged, proj_hidden, preferred_element_type=jnp.float32)
            ).astype(jnp.bfloat16)
            return jnp.einsum("ik,ck->ci", hidden, score_weight, preferred_element_type=jnp.float32)

        def empty_block(block_rows):
            return jnp.zeros((2, BLOCK), jnp.float32)

        return lax.cond(is_live, score_block, empty_block, block_rows)

    logits = lax.map(
        score_slot, (arrived.reshape(slot_count, BLOCK, model_width), request_of, live_slots)
    )
    logits = logits.reshape(requests, per_scorer, 2, BLOCK)
    decays = jnp.exp(
        -item_ages.astype(jnp.float32).reshape(requests, per_scorer, BLOCK) / AGE_SCALE
    )
    blended = decays * logits[:, :, 0] + (1.0 - decays) * logits[:, :, 1]
    row_number = (my_shard * per_scorer + jnp.arange(per_scorer, dtype=jnp.int32))[
        None, :, None
    ] * BLOCK + jnp.arange(BLOCK, dtype=jnp.int32)[None, None, :]
    kept_rows = row_number < candidate_count[:, None, None]
    return jnp.where(kept_rows, blended, 0.0).reshape(requests, per_scorer * BLOCK)


def solution(mesh):
    return jax.shard_map(
        local,
        mesh=mesh,
        in_specs=(
            P("req", "cand", None),
            P("req"),
            P("req"),
            P("req", None),
            P("req", None),
            P("cand", None, None),
            P("req", "cand"),
            P("req", None),
            P("req", None),
            P("req", None),
            P("req", None),
            P(),
            P(),
        ),
        out_specs=P("req", "cand"),
        check_vma=False,
    )
```

profile of v0, /device:TPU:3, one launch (start us, length us, event | category | flops | bytes accessed | tf_op | source)
XLA Modules:
  0.0 1650.8 jit_solution(6157410167003567485)
XLA Ops:
  25.0 22.5 %all-gather.5.cloned.1.call-done = bf16[1024,2048]{1,0:T(8,128)(2,1)} async-done(((bf16[128,2048]{1,0:T(8,128)(2,1)}), bf16[1024,2048]{1,0:T(8,128)(2,1)}) %all-gather.5.cloned.1.call-update) | async-done | bytes 4194320 | tf_op jit(solution)/shard_map/all_gather | solution.py:29
  68.9 19.3 %all-gather.9.cloned.1.call-done = bf16[1024,2048]{1,0:T(8,128)(2,1)} async-done(((bf16[128,2048]{1,0:T(8,128)(2,1)}), bf16[1024,2048]{1,0:T(8,128)(2,1)}) %all-gather.9.cloned.1.call-update) | async-done | bytes 4194320 | tf_op jit(solution)/shard_map/all_gather | solution.py:30
  92.3 277.3 %all-gather.7.cloned.1.call-done = bf16[8,256,2048]{2,0,1:T(8,128)(2,1)} async-done(((bf16[8,64,2048]{2,0,1:T(8,128)(2,1)}), bf16[8,256,2048]{2,0,1:T(8,128)(2,1)}) %all-gather.7.cloned.1.call-update) | async-done | bytes 8388624 | tf_op jit(solution)/shard_map/all_gather | solution.py:76
  382.2 139.2 %all-to-all-done = bf16[4,16,128,1024]{3,2,1,0:T(8,128)(2,1)} async-done(((bf16[4,16,128,1024]{3,2,1,0:T(8,128)(2,1)}), bf16[4,16,128,1024]{3,2,1,0:T(8,128)(2,1)}, u32[]{:S(2)}, u32[]{:S(2)}) %all-to-all-start) | async-done | bytes 16777248 | tf_op jit(solution)/shard_map/all_to_all | solution.py:60
  534.9 1108.1 %while.11 = (s32[]{:T(128)}, f32[64,2,128]{2,1,0:T(2,128)S(1)}, pred[64]{0:T(512)(128)(4,1)S(1)}, bf16[8,256,2048]{1,2,0:T(8,128)(2,1)}, s32[8]{0:T(128)S(1)}, /...) while((s32[]{:T(128)}, f32[64,2,128]{2,1,0:T(2,128)S(1)}, ...), condition=%wide.region_9.10_spmd.clone, body=%wide.region_4.9_spmd.clone.sunk | while | flops 1011778432 | bytes 19286676 | solution.py:123
  536.3 16.0 conditional.3
  553.6 15.9 conditional.3
  570.9 15.9 conditional.3
  588.2 15.9 conditional.3
  605.6 15.9 conditional.3
  622.9 15.9 conditional.3
  640.2 15.9 conditional.3
  657.5 15.9 conditional.3
  674.8 15.9 conditional.3
  692.1 15.9 conditional.3
  709.4 15.9 conditional.3
  726.8 15.9 conditional.3
  744.1 15.9 conditional.3
  761.4 15.9 conditional.3
  778.7 15.9 conditional.3
  796.0 15.9 conditional.3
  813.3 15.9 conditional.3
  830.6 15.9 conditional.3
  848.0 15.9 conditional.3
  865.3 15.9 conditional.3
  882.6 15.9 conditional.3
  899.9 15.9 conditional.3
  917.2 15.9 conditional.3
  934.5 15.9 conditional.3
  951.8 15.9 conditional.3
  969.2 15.9 conditional.3
  986.5 15.9 conditional.3
  1003.8 15.9 conditional.3
  1021.1 15.9 conditional.3
  1038.4 15.9 conditional.3
  1055.7 15.9 conditional.3
  1073.0 15.9 conditional.3
  1090.3 15.9 conditional.3
  1107.7 15.9 conditional.3
  1125.0 15.9 conditional.3
  1142.3 15.9 conditional.3
  1159.6 15.9 conditional.3
  1176.9 15.9 conditional.3
  1194.2 15.9 conditional.3
  1211.5 15.9 conditional.3
  1228.9 15.9 conditional.3
  1246.2 15.9 conditional.3
  1263.5 15.9 conditional.3
  1280.8 15.9 conditional.3
  1298.1 15.9 conditional.3
  1315.4 15.9 conditional.3
  1332.7 15.9 conditional.3
  1350.1 15.9 conditional.3
  1367.4 15.9 conditional.3
  1384.7 15.9 conditional.3
  1402.0 15.9 conditional.3
  1419.3 15.9 conditional.3
  1436.6 15.9 conditional.3
  1453.9 15.9 conditional.3
  1471.2 15.9 conditional.3
  1488.6 15.9 conditional.3
  1505.9 15.9 conditional.3
  1523.2 15.9 conditional.3
  1609.8 15.9 conditional.3
  (1475 shorter events, 1045.5 us)
Async XLA Ops:
  6.5 40.9 %all-gather.5.cloned.1.call-start = ((), (), s32[]{:S(2)}) async-start(), calls=%async_computation.1 | async-start | bytes 4718592 | tf_op jit(solution)/shard_map/all_gather | solution.py:29
  17.0 30.5 %copy-start.7 = (bf16[8,64,1024]{2,1,0:T(8,128)(2,1)S(1)}, bf16[8,64,1024]{2,1,0:T(8,128)(2,1)}, u32[]{:S(2)}) copy-start(bf16[8,64,1024]{2,1,0:T(8,128)(2,1)} %param.17) | copy-start | bytes 3145732
  17.0 504.5 %all-to-all-start = ((bf16[4,16,128,1024]{3,2,1,0:T(8,128)(2,1)}), bf16[4,16,128,1024]{3,2,1,0:T(8,128)(2,1)}, u32[]{:S(2)}, u32[]{:S(2)}) async-start(bf16[4,16,128,1024]{3,2,1,0:T(8,128)(2,1)} %bitcast.105), calls=%async_computation | async-start | bytes 33554432 | tf_op jit(solution)/shard_map/all_to_all | solution.py:60
  24.2 64.0 %all-gather.9.cloned.1.call-start = ((), (), s32[]{:S(2)}) async-start(), calls=%async_computation.3 | async-start | bytes 4718592 | tf_op jit(solution)/shard_map/all_gather | solution.py:30
  25.0 344.6 %all-gather.7.cloned.1.call-start = ((), (), s32[]{:S(2)}) async-start(), calls=%async_computation.2 | async-start | bytes 10485760 | tf_op jit(solution)/shard_map/all_gather | solution.py:76
  55.0 479.9 %all-gather.11.cloned.1.call-start = ((), (), s32[]{:S(2)}) async-start(), calls=%async_computation.4 | async-start | bytes 2359296 | tf_op jit(solution)/shard_map/all_gather | solution.py:31
  521.4 13.5 copy-start.5
  521.5 13.5 copy-start.8
  521.5 13.5 copy-start.9
  534.9 1108.2 %copy-start.4 = (s32[8,1024]{1,0:T(8,128)S(1)}, s32[8,1024]{1,0:T(8,128)}, u32[]{:S(2)}) copy-start(s32[8,1024]{1,0:T(8,128)} %param.23) | copy-start | bytes 98308
  558.7 4.6 copy-start.2
  576.0 4.6 copy-start.2
  593.3 4.6 copy-start.2
  610.6 4.6 copy-start.2
  627.9 4.6 copy-start.2
  645.2 4.6 copy-start.2
  662.6 4.6 copy-start.2
  679.9 4.6 copy-start.2
  697.2 4.6 copy-start.2
  714.5 4.6 copy-start.2
  731.8 4.6 copy-start.2
  749.1 4.6 copy-start.2
  766.4 4.6 copy-start.2
  783.8 4.6 copy-start.2
  801.1 4.6 copy-start.2
  818.4 4.6 copy-start.2
  835.7 4.6 copy-start.2
  853.0 4.6 copy-start.2
  870.3 4.6 copy-start.2
  887.6 4.6 copy-start.2
  904.9 4.6 copy-start.2
  922.3 4.6 copy-start.2
  939.6 4.6 copy-start.2
  956.9 4.6 copy-start.2
  974.2 4.6 copy-start.2
  991.5 4.6 copy-start.2
  1008.8 4.6 copy-start.2
  1026.1 4.6 copy-start.2
  1043.5 4.6 copy-start.2
  1060.8 4.6 copy-start.2
  1078.1 4.6 copy-start.2
  1095.4 4.6 copy-start.2
  1112.7 4.6 copy-start.2
  1130.0 4.6 copy-start.2
  1147.3 4.6 copy-start.2
  1164.7 4.6 copy-start.2
  1182.0 4.6 copy-start.2
  1199.3 4.6 copy-start.2
  1216.6 4.6 copy-start.2
  1233.9 4.6 copy-start.2
  1251.2 4.6 copy-start.2
  1268.5 4.6 copy-start.2
  1285.8 4.6 copy-start.2
  1303.2 4.6 copy-start.2
  1320.5 4.6 copy-start.2
  1337.8 4.6 copy-start.2
  1355.1 4.6 copy-start.2
  1372.4 4.6 copy-start.2
  1407.0 4.6 copy-start.2
  1424.4 4.6 copy-start.2
  1493.6 4.6 copy-start.2
  1510.9 4.6 copy-start.2
  1562.9 4.6 copy-start.2
  1580.2 4.6 copy-start.2
  (14 other events, 57.2 us)
Sparse Core Ops, SparseCore 0:
  9.2 38.2 all-gather.4
  49.4 38.7 all-gather.8
  89.8 279.6 all-gather.6
  371.3 143.0 all-gather.10
where the time goes:
time: 1670 us; the launch traced here: 1650 us
  matrix products  567 us (34%)
  waiting for transfers between devices  460 us (28%)
  local copies, waits for them, and re-layouts  328 us (20%)
  loops' own time  214 us (13%)
  other arithmetic  48.9 us (3%)
    all_gather x1, waiting for transfers between devices, local(): projected = lax.all_gather(local_pairs, 'cand', axis=1, tiled=True)  277 us
    dot_general x64, matrix products, score_block(): jnp.dot(block_rows, query_weight, preferred_element_type=jnp.float32)  185 us
    another operation x64, loops' own time, score_slot(): return lax.cond(is_live, score_block, empty_block, block_rows)  169 us
    dot_general x64, matrix products, score_block(): jnp.dot(merged, proj_hidden, preferred_element_type=jnp.float32)  164 us
    all_to_all x1, waiting for transfers between devices, local(): lax.all_to_all(outgoing, 'cand', split_axis=0, concat_axis=0, tiled=True)  139 us
    dot_general x64, matrix products, score_block(): jnp.einsum('hip,phd->ihd', weights, value_rows, preferred_element_type=jn...  116 us
    dot_general x64, matrix products, score_block(): jnp.dot(block_rows, gate_weight, preferred_element_type=jnp.float32)  89.4 us
    dynamic_slice x128, local copies, waits for them, and re-layouts, local(): lax.map(score_slot, (arrived.reshape(slot_count, BLOCK, model_width), req...  83.3 us
  transfers between devices with their start and end apart: 5, of which 4 were waited for; matrix products, arithmetic and copies ran while one was open for 3% of the time, Pallas kernels for 0%

commit v1 on v0

--- a/solution.py
+++ b/solution.py
@@ -8,6 +8,28 @@
 BLOCK = 128
 EPSILON = 1e-05
 AGE_SCALE = 48.0
+
+
+def laid_out(blocks, dim):
+    blocks = jnp.moveaxis(blocks, 0, dim)
+    shape = blocks.shape
+    return blocks.reshape(*shape[:dim], shape[dim] * shape[dim + 1], *shape[dim + 2 :])
+
+
+def gather_around(shard, axis, dim):
+    size = lax.axis_size(axis)
+    pairs = [(i, (i + 1) % size) for i in range(size)]
+    back = [(b, a) for a, b in pairs]
+    lower, upper = ([], [])
+    for hop in range(size - 1):
+        if hop % 2 == 0:
+            lower.append(lax.ppermute(lower[-1] if lower else shard, axis, pairs))
+        else:
+            upper.append(lax.ppermute(upper[-1] if upper else shard, axis, back))
+    parts = jnp.stack([*lower[::-1], shard, *upper])
+    shift = lax.axis_index(axis) - len(lower)
+    parts = parts[(jnp.arange(size) - shift) % size]
+    return laid_out(parts, dim)
 
 
 def local(
@@ -73,7 +95,7 @@
         jnp.dot(history.reshape(-1, model_width), proj_history, preferred_element_type=jnp.float32)
     ).astype(jnp.bfloat16)
     local_pairs = local_pairs.reshape(requests, -1, 2 * model_width)
-    projected = lax.all_gather(local_pairs, "cand", axis=1, tiled=True)
+    projected = gather_around(local_pairs, "cand", 1)
     history_total = projected.shape[1]
     positions = jnp.arange(history_total, dtype=jnp.int32)
     query_weight = proj_candidate[:, :model_width]

time: 1670 us -> 1700 us (1.018)
  starting transfers between devices: 7.37 us -> 143 us
  waiting for transfers between devices: 460 us -> 334 us
    ppermute x0 -> x3, waiting for transfers between devices: none -> 293 us  [the longest x2 293 us: gather_around(): lower.append(lax.ppermute(lower[-1] if lower else shard, axis, pairs))]
    all_gather x1 -> x0, waiting for transfers between devices: 277 us -> none  [local(): projected = lax.all_gather(local_pairs, 'cand', axis=1, tiled=True)]
    all_to_all x1, waiting for transfers between devices: 139 us -> 0.01 us  [local(): lax.all_to_all(outgoing, 'cand', split_axis=0, concat_axis=0, tiled=True)]
    ppermute x0 -> x3, starting transfers between devices: none -> 135 us  [the longest x2 133 us: gather_around(): lower.append(lax.ppermute(lower[-1] if lower else shard, axis, pairs))]
    all_gather x1, waiting for transfers between devices: 19.3 us -> 0.01 us  [local(): lax.all_gather(candidate_weight, 'req', axis=0, tiled=True)]
    all_gather x1, waiting for transfers between devices: 22.5 us -> 39.6 us  [local(): lax.all_gather(history_weight, 'req', axis=0, tiled=True)]
  transfers between devices with their start and end apart: 5 -> 7, of which waited for: 4 -> 3; matrix products, arithmetic and copies ran while one was open for 3% -> 4% of each run, Pallas kernels for 0% -> 0%
where the time goes in v1:
time: 1700 us; the launch traced here: 1680 us
  matrix products  569 us (33%)
  local copies, waits for them, and re-layouts  344 us (20%)
  waiting for transfers between devices  334 us (20%)
  loops' own time  201 us (12%)
  starting transfers between devices  143 us (8%)
  other arithmetic  65.4 us (4%)
    ppermute x2, waiting for transfers between devices, gather_around(): lower.append(lax.ppermute(lower[-1] if lower else shard, axis, pairs))  293 us
    dot_general x64, matrix products, score_block(): jnp.dot(block_rows, query_weight, preferred_element_type=jnp.float32)  185 us
    dot_general x64, matrix products, score_block(): jnp.dot(merged, proj_hidden, preferred_element_type=jnp.float32)  163 us
    another operation x64, loops' own time, score_slot(): return lax.cond(is_live, score_block, empty_block, block_rows)  161 us
    ppermute x2, starting transfers between devices, gather_around(): lower.append(lax.ppermute(lower[-1] if lower else shard, axis, pairs))  133 us
    dot_general x64, matrix products, score_block(): jnp.einsum('hip,phd->ihd', weights, value_rows, preferred_element_type=jn...  116 us
    dot_general x64, matrix products, score_block(): jnp.dot(block_rows, gate_weight, preferred_element_type=jnp.float32)  89.4 us
    squeeze x64, local copies, waits for them, and re-layouts, score_block(): pair_rows = lax.dynamic_index_in_dim(projected, request, 0, keepdims=False)  83.2 us
  transfers between devices with their start and end apart: 7, of which 3 were waited for; matrix products, arithmetic and copies ran while one was open for 4% of the time, Pallas kernels for 0%

profile of v1, /device:TPU:3, one launch (start us, length us, event | category | flops | bytes accessed | tf_op | source)
XLA Modules:
  0.0 1682.0 jit_solution(1806199480560366053)
XLA Ops:
  25.0 39.6 %all-gather.4.cloned.1.call-done = bf16[1024,2048]{1,0:T(8,128)(2,1)} async-done(((bf16[128,2048]{1,0:T(8,128)(2,1)}), bf16[1024,2048]{1,0:T(8,128)(2,1)}) %all-gather.4.cloned.1.call-update) | async-done | bytes 4194320 | tf_op jit(solution)/shard_map/all_gather | solution.py:51
  74.2 267.6 %collective-permute-done = bf16[8,64,2048]{2,1,0:T(8,128)(2,1)} collective-permute-done((bf16[8,64,2048]{2,1,0:T(8,128)(2,1)}, bf16[8,64,2048]{2,1,0:T(8,128)(2,1)}, u32[]{:S(2)}, u32[]{:S(2)}) %collective-permute-start) | collective-permute-done | bytes 2097184 | tf_op jit(solution)/shard_map/ppermute | solution.py:26
  341.8 132.2 %collective-permute-start.1 = (bf16[8,64,2048]{2,1,0:T(8,128)(2,1)}, bf16[8,64,2048]{2,1,0:T(8,128)(2,1)}, u32[]{:S(2)}, u32[]{:S(2)}) collective-permute-start(bf16[8,64,2048]{2,1,0:T(8,128)(2,1)} %collective-permute-done), channel_id=1, source_target_pairs={{0,1},{1,2},{2,3},{3,0},{4,5},{5,6},{6,7},{7,4},{8,9},{9,10},{10,1... | collective-permute-start | bytes 6291464 | tf_op jit(solution)/shard_map/ppermute | solution.py:26
  492.6 25.2 %collective-permute-done.1 = bf16[8,64,2048]{2,1,0:T(8,128)(2,1)} collective-permute-done((bf16[8,64,2048]{2,1,0:T(8,128)(2,1)}, bf16[8,64,2048]{2,1,0:T(8,128)(2,1)}, u32[]{:S(2)}, u32[]{:S(2)}) %collective-permute-start.1) | collective-permute-done | bytes 2097184 | tf_op jit(solution)/shard_map/ppermute | solution.py:26
  576.9 1097.3 %while.11 = (s32[]{:T(128)}, f32[64,2,128]{2,1,0:T(2,128)S(1)}, pred[64]{0:T(512)(128)(4,1)S(1)}, bf16[8,256,2048]{1,2,0:T(8,128)(2,1)}, s32[8]{0:T(128)S(1)}, /...) while((s32[]{:T(128)}, f32[64,2,128]{2,1,0:T(2,128)S(1)}, ...), condition=%wide.region_9.10_spmd.clone, body=%wide.region_4.9_spmd.clone.sunk | while | flops 1011778432 | bytes 19286676 | solution.py:145
  578.2 15.9 conditional.3
  595.4 15.9 conditional.3
  612.5 15.9 conditional.3
  629.7 15.9 conditional.3
  646.8 15.9 conditional.3
  663.9 15.9 conditional.3
  681.1 15.9 conditional.3
  698.2 15.9 conditional.3
  715.4 15.9 conditional.3
  732.5 15.9 conditional.3
  749.7 15.9 conditional.3
  766.8 15.9 conditional.3
  784.0 15.9 conditional.3
  801.1 15.9 conditional.3
  818.3 15.9 conditional.3
  835.4 15.9 conditional.3
  852.5 15.9 conditional.3
  869.7 15.9 conditional.3
  886.8 15.9 conditional.3
  904.0 15.9 conditional.3
  921.1 15.9 conditional.3
  938.3 15.9 conditional.3
  955.4 15.9 conditional.3
  972.6 15.9 conditional.3
  989.7 15.9 conditional.3
  1006.9 15.9 conditional.3
  1024.0 15.9 conditional.3
  1041.1 15.9 conditional.3
  1058.3 15.9 conditional.3
  1075.4 15.9 conditional.3
  1092.6 15.9 conditional.3
  1109.7 15.9 conditional.3
  1126.9 15.9 conditional.3
  1144.0 15.9 conditional.3
  1161.2 15.9 conditional.3
  1178.3 15.9 conditional.3
  1195.4 15.9 conditional.3
  1212.6 15.9 conditional.3
  1229.7 15.9 conditional.3
  1246.9 15.9 conditional.3
  1264.0 15.9 conditional.3
  1281.2 15.9 conditional.3
  1298.3 15.9 conditional.3
  1315.5 15.9 conditional.3
  1332.6 15.9 conditional.3
  1349.8 15.9 conditional.3
  1366.9 15.9 conditional.3
  1384.0 15.9 conditional.3
  1401.2 15.9 conditional.3
  1418.3 15.9 conditional.3
  1435.5 15.9 conditional.3
  1452.6 15.9 conditional.3
  1469.8 15.9 conditional.3
  1486.9 15.9 conditional.3
  1504.1 15.9 conditional.3
  1521.2 15.9 conditional.3
  1538.4 15.9 conditional.3
  1589.8 15.9 conditional.3
  1606.9 15.9 conditional.3
  (1485 shorter events, 1082.5 us)
Async XLA Ops:
  16.3 48.2 %copy-start.7 = (bf16[8,64,1024]{2,1,0:T(8,128)(2,1)S(1)}, bf16[8,64,1024]{2,1,0:T(8,128)(2,1)}, u32[]{:S(2)}) copy-start(bf16[8,64,1024]{2,1,0:T(8,128)(2,1)} %param.17) | copy-start | bytes 3145732
  16.3 547.1 %all-to-all-start = ((bf16[4,16,128,1024]{3,2,1,0:T(8,128)(2,1)}), bf16[4,16,128,1024]{3,2,1,0:T(8,128)(2,1)}, u32[]{:S(2)}, u32[]{:S(2)}) async-start(bf16[4,16,128,1024]{3,2,1,0:T(8,128)(2,1)} %bitcast.114), calls=%async_computation | async-start | bytes 33554432 | tf_op jit(solution)/shard_map/all_to_all | solution.py:82
  23.5 41.1 %all-gather.4.cloned.1.call-start = ((), (), s32[]{:S(2)}) async-start(), calls=%async_computation.1 | async-start | bytes 4718592 | tf_op jit(solution)/shard_map/all_gather | solution.py:51
  24.2 464.3 %all-gather.6.cloned.1.call-start = ((), (), s32[]{:S(2)}) async-start(), calls=%async_computation.2 | async-start | bytes 4718592 | tf_op jit(solution)/shard_map/all_gather | solution.py:52
  24.9 552.0 %all-gather.8.cloned.1.call-start = ((), (), s32[]{:S(2)}) async-start(), calls=%async_computation.3 | async-start | bytes 2359296 | tf_op jit(solution)/shard_map/all_gather | solution.py:53
  64.6 409.6 %copy-start.6 = (s32[8]{0:T(128)S(1)}, s32[8]{0:T(128)}, u32[]{:S(2)}) copy-start(s32[8]{0:T(128)} %param.19) | copy-start | bytes 100
  64.6 410.1 %copy-start.3 = (bf16[128,256]{1,0:T(8,128)(2,1)S(1)}, bf16[128,256]{1,0:T(8,128)(2,1)}, u32[]{:S(2)}) copy-start(bf16[128,256]{1,0:T(8,128)(2,1)} %param.27) | copy-start | bytes 196612
  71.0 270.9 %collective-permute-start = (bf16[8,64,2048]{2,1,0:T(8,128)(2,1)}, bf16[8,64,2048]{2,1,0:T(8,128)(2,1)}, u32[]{:S(2)}, u32[]{:S(2)}) collective-permute-start(bf16[8,64,2048]{2,1,0:T(8,128)(2,1)} %bitcast.13), channel_id=1, source_target_pairs={{0,1},{1,2},{2,3},{3,0},{4,5},{5,6},{6,7},{7,4},{8,9},{9,10},{10,1... | collective-permute-start | bytes 6291464 | tf_op jit(solution)/shard_map/ppermute | solution.py:26
  72.2 420.4 %collective-permute-start.2 = (bf16[8,64,2048]{2,1,0:T(8,128)(2,1)}, bf16[8,64,2048]{2,1,0:T(8,128)(2,1)}, u32[]{:S(2)}, u32[]{:S(2)}) collective-permute-start(bf16[8,64,2048]{2,1,0:T(8,128)(2,1)} %bitcast.13), channel_id=1, source_target_pairs={{1,0},{2,1},{3,2},{0,3},{5,4},{6,5},{7,6},{4,7},{9,8},{10,9},{11,1... | collective-permute-start | bytes 6291464 | tf_op jit(solution)/shard_map/ppermute | solution.py:28
  341.8 175.9 %collective-permute-start.1 = (bf16[8,64,2048]{2,1,0:T(8,128)(2,1)}, bf16[8,64,2048]{2,1,0:T(8,128)(2,1)}, u32[]{:S(2)}, u32[]{:S(2)}) collective-permute-start(bf16[8,64,2048]{2,1,0:T(8,128)(2,1)} %collective-permute-done), channel_id=1, source_target_pairs={{0,1},{1,2},{2,3},{3,0},{4,5},{5,6},{6,7},{7,4},{8,9},{9,10},{10,1... | collective-permute-start | bytes 6291464 | tf_op jit(solution)/shard_map/ppermute | solution.py:26
  563.5 13.5 copy-start.5
  563.5 13.5 copy-start.8
  563.5 13.5 copy-start.9
  576.9 1097.4 %copy-start.4 = (s32[8,1024]{1,0:T(8,128)S(1)}, s32[8,1024]{1,0:T(8,128)}, u32[]{:S(2)}) copy-start(s32[8,1024]{1,0:T(8,128)} %param.23) | copy-start | bytes 98308
  600.2 4.7 copy-start.2
  617.3 4.7 copy-start.2
  634.5 4.7 copy-start.2
  668.8 4.7 copy-start.2
  685.9 4.7 copy-start.2
  703.1 4.7 copy-start.2
  720.2 4.7 copy-start.2
  737.4 4.7 copy-start.2
  771.7 4.7 copy-start.2
  788.8 4.7 copy-start.2
  805.9 4.7 copy-start.2
  823.1 4.7 copy-start.2
  840.2 4.7 copy-start.2
  874.5 4.7 copy-start.2
  891.7 4.7 copy-start.2
  908.8 4.7 copy-start.2
  926.0 4.7 copy-start.2
  943.1 4.7 copy-start.2
  994.5 4.7 copy-start.2
  1011.7 4.7 copy-start.2
  1028.8 4.7 copy-start.2
  1046.0 4.7 copy-start.2
  1063.1 4.7 copy-start.2
  1097.4 4.7 copy-start.2
  1114.6 4.7 copy-start.2
  1131.7 4.7 copy-start.2
  1148.9 4.7 copy-start.2
  1166.0 4.7 copy-start.2
  1200.3 4.7 copy-start.2
  1217.4 4.7 copy-start.2
  1234.6 4.7 copy-start.2
  1251.7 4.7 copy-start.2
  1268.9 4.7 copy-start.2
  1320.3 4.7 copy-start.2
  1337.4 4.7 copy-start.2
  1354.6 4.7 copy-start.2
  1371.7 4.7 copy-start.2
  1388.9 4.7 copy-start.2
  1423.2 4.7 copy-start.2
  1440.3 4.7 copy-start.2
  1457.5 4.7 copy-start.2
  1474.6 4.7 copy-start.2
  1491.8 4.7 copy-start.2
  1526.0 4.7 copy-start.2
  1543.2 4.7 copy-start.2
  1560.3 4.7 copy-start.2
  1577.5 4.7 copy-start.2
  1594.6 4.7 copy-start.2
  1646.1 4.7 copy-start.2
  1663.2 4.7 copy-start.2
  (16 other events, 70.0 us)
Sparse Core Ops, SparseCore 0:
  26.1 38.3 all-gather.3
  66.4 36.5 all-gather.5
  474.1 29.4 all-gather.7
